TPU v7x, 256 devices: a whole 4x4x8 slice. The times are simulated.
256 devices in a mesh: dp: 16 (over y_hi, z), fsdp: 16 (over y_lo, x, core).
Axes of the slice: x: 4, y: 4 (y_hi: 2, y_lo: 2; y = y_hi * 2 + y_lo), z: 8, core: 2. Of those that a mesh axis runs over, the one named last changes fastest.
Arguments:
- item_tokens: bfloat16 [131072, 4096], P(('dp', 'fsdp')), may hold values from -6 to 6
- item_lengths: int32 [1024], P(('dp', 'fsdp')), may hold values from 1 to 128
- item_gain: float32 [4096], replicated, may hold values from 0.1 to 1.9
- user_source: int32 [65536, 1], P(('dp', 'fsdp')), may hold values from 0 to 15; in each aligned block of 256 rows (0 to 255, 256 to 511, ...) at most 24 rows name the same one
- user_slot: int32 [65536], P(('dp', 'fsdp')), may hold values from 0 to 3
- user_lengths: int32 [256], P(('dp', 'fsdp')), may hold values from 1 to 256
- user_gain: float32 [4096], replicated, may hold values from 0.1 to 1.9
- key_weight: bfloat16 [4096, 1024], P('fsdp'), may hold values from -0.09375 to 0.09375
- key_grad: bfloat16 [65536, 1024], P(('dp', 'fsdp')), may hold values from -6 to 6
Outputs:
- keys: bfloat16 [65536, 1024], P(('dp', 'fsdp'))
- weight_grad: float32 [4096, 1024], P('fsdp')
- token_grads: bfloat16 [131072, 4096], P(('dp', 'fsdp'))
Inputs may be any that keep to these rules, and one draw needn't show every extreme that they name: `user_source`: among the 256 positions of one device, no source index appears more than 24 times, and in every draw some device reaches 24 for some source.
All inputs are finite; a program needn't handle non-finite values.
Results may differ from a plain program's by a relative error of at most 0.0057.
Values may be sent and summed in bfloat16 or wider, within the bound.
A program may use at most 128 MiB of HBM per device.

v0:
```python
import jax
import jax.numpy as jnp
from jax import lax
from jax.sharding import PartitionSpec as P

EPS = 1e-05


def rms_scale(vector, gain_row):
    return vector * lax.rsqrt(jnp.mean(vector * vector, axis=-1, keepdims=True) + EPS) * gain_row


def pool_items(token_block, valid_mask, item_sizes, gain_row):
    normed = rms_scale(token_block, gain_row)
    return jnp.sum(normed * valid_mask[:, :, None], axis=1) / item_sizes[:, None]


def local(
    item_tokens,
    item_lengths,
    item_gain,
    user_source,
    user_slot,
    user_lengths,
    user_gain,
    key_weight,
    key_grad,
):
    item_count = item_lengths.shape[0]
    block_rows = item_tokens.shape[0] // item_count
    model_width = item_tokens.shape[1]
    group_count = lax.axis_size("dp")
    stacked_tokens = item_tokens.reshape(item_count, block_rows, model_width)
    valid_mask = (
        lax.broadcasted_iota(jnp.int32, (item_count, block_rows), 1) < item_lengths[:, None]
    ).astype(jnp.float32)
    item_sizes = item_lengths.astype(jnp.float32)

    def pooling(tokens_float):
        return pool_items(tokens_float, valid_mask, item_sizes, item_gain)

    pooled, pool_back = jax.vjp(pooling, stacked_tokens.astype(jnp.float32))
    item_emb = pooled.astype(jnp.bfloat16)
    weights = lax.all_gather(key_weight, "fsdp", axis=0, tiled=True)
    row_count = user_slot.shape[0]
    source = user_source[:, 0]
    seq_count = user_lengths.shape[0]
    seq_rows = row_count // seq_count
    alive_mask = (
        lax.broadcasted_iota(jnp.int32, (seq_count, seq_rows), 1) < user_lengths[:, None]
    ).reshape(row_count, 1)
    capacity = 3 * row_count // (2 * group_count)
    source_hot = (
        source[:, None] == lax.broadcasted_iota(jnp.int32, (row_count, group_count), 1)
    ).astype(jnp.int32)
    before = jnp.cumsum(source_hot, axis=0) - source_hot
    slot_rank = jnp.sum(before * source_hot, axis=1)
    bucket = source * capacity + slot_rank
    request = (
        jnp.zeros((group_count * capacity,), jnp.int32)
        .at[bucket]
        .set(user_slot)
        .reshape(group_count, capacity)
    )
    requested = lax.all_to_all(request, "dp", split_axis=0, concat_axis=0, tiled=True)
    outgoing = jnp.take(item_emb, requested.reshape(-1), axis=0).reshape(
        group_count, capacity, model_width
    )
    arrived = lax.all_to_all(outgoing, "dp", split_axis=0, concat_axis=0, tiled=True)
    fetched = jnp.take(arrived.reshape(group_count * capacity, model_width), bucket, axis=0)
    embedded = jnp.where(alive_mask, fetched, jnp.zeros_like(fetched))

    def normalize(vector):
        return rms_scale(vector, user_gain)

    scaled, norm_back = jax.vjp(normalize, embedded.astype(jnp.float32))
    hidden = scaled.astype(jnp.bfloat16)
    key_rows = jnp.dot(hidden, weights, preferred_element_type=jnp.float32).astype(jnp.bfloat16)
    hidden_grad = lax.dot_general(
        key_grad, weights, (((1,), (1,)), ((), ())), preferred_element_type=jnp.float32
    )
    (embed_grad,) = norm_back(hidden_grad)
    pos_grad = jnp.where(alive_mask, embed_grad, jnp.zeros_like(embed_grad)).astype(jnp.bfloat16)
    weight_shard = lax.psum_scatter(
        lax.dot_general(
            hidden, key_grad, (((0,), (0,)), ((), ())), preferred_element_type=jnp.float32
        ),
        "fsdp",
        scatter_dimension=0,
        tiled=True,
    )
    weight_grad = lax.psum(weight_shard, "dp")
    scattered = (
        jnp.zeros((group_count * capacity, model_width), jnp.bfloat16)
        .at[bucket]
        .set(pos_grad)
        .reshape(group_count, capacity, model_width)
    )
    returned = lax.all_to_all(scattered, "dp", split_axis=0, concat_axis=0, tiled=True)
    item_table = (
        requested.reshape(1, group_count * capacity)
        == lax.broadcasted_iota(jnp.int32, (item_count, group_count * capacity), 0)
    ).astype(jnp.bfloat16)
    item_grad = jnp.dot(
        item_table,
        returned.reshape(group_count * capacity, model_width),
        preferred_element_type=jnp.float32,
    )
    (tokens_back,) = pool_back(item_grad)
    token_grads = tokens_back.reshape(item_count * block_rows, model_width).astype(jnp.bfloat16)
    return (key_rows, weight_grad, token_grads)


def solution(mesh):
    in_specs = (
        P(("dp", "fsdp"), None),
        P(("dp", "fsdp")),
        P(),
        P(("dp", "fsdp"), None),
        P(("dp", "fsdp")),
        P(("dp", "fsdp")),
        P(),
        P("fsdp", None),
        P(("dp", "fsdp"), None),
    )
    out_specs = (P(("dp", "fsdp"), None), P("fsdp", None), P(("dp", "fsdp"), None))
    return jax.shard_map(local, mesh=mesh, in_specs=in_specs, out_specs=out_specs, check_vma=False)
```

profile of v0, /device:TPU:2, one launch (start us, length us, event | category | flops | bytes accessed | tf_op | source)
XLA Modules:
  0.0 447.3 jit_solution(16365344587193851670)
XLA Ops:
  7.2 0.7 all-gather.2.cloned.1.call-update
  7.9 0.7 fusion.19
  8.6 0.6 reduce-window.6
  9.4 0.8 fusion.18
  10.2 0.7 and_reduce_fusion
  10.9 1.6 scatter_custom_fusion
  12.4 0.7 all_to_all.12
  13.1 11.2 %all-to-all-start = ((s32[16,1,24]{2,1,0:T(1,128)}), s32[16,1,24]{2,1,0:T(1,128)S(1)}, u32[]{:S(2)}, u32[]{:S(2)}) async-start(s32[16,1,24]{2,1,0:T(1,128)} %all_to_all.12), calls=%async_computation | async-start | bytes 16384 | tf_op jit(solution)/shard_map/all_to_all | solution.py:65
  24.4 0.8 convert_element_type.59
  25.2 1.0 fusion.27
  26.2 3.1 multiply_reduce_fusion.1
  29.3 2.1 multiply_reduce_fusion
  31.5 2.8 all-to-all-done
  34.3 0.5 broadcast.177
  34.8 0.7 reduce.13
  35.6 4.0 gather_fusion
  39.5 4.0 broadcast_select_fusion
  43.5 6.9 %all-to-all-start.1 = ((bf16[16,24,4096]{2,1,0:T(8,128)(2,1)}), bf16[16,24,4096]{2,1,0:T(8,128)(2,1)}, u32[]{:S(2)}, u32[]{:S(2)}) async-start(bf16[16,24,4096]{2,1,0:T(8,128)(2,1)} %broadcast_select_fusion), calls=%async_computation.1 | async-start | bytes 6291456 | tf_op jit(solution)/shard_map/all_to_all | solution.py:69
  50.4 0.2 reduce-scatter.2.cloned.1.call-start
  51.3 71.9 %all-to-all-done.1 = bf16[16,24,4096]{2,1,0:T(8,128)(2,1)} async-done(((bf16[16,24,4096]{2,1,0:T(8,128)(2,1)}), bf16[16,24,4096]{2,1,0:T(8,128)(2,1)}, u32[]{:S(2)}, u32[]{:S(2)}) %all-to-all-start.1) | async-done | bytes 3145760 | tf_op jit(solution)/shard_map/all_to_all | solution.py:69
  123.2 6.2 %gather_fusion.1 = bf16[256,4096]{1,0:T(8,128)(2,1)S(1)} fusion(bf16[384,4096]{1,0:T(8,128)(2,1)} %bitcast.10, s32[1024]{0:T(1024)S(1)} %pad_clamp_fusion), kind=kCustom, calls=%fused_computation.1 | custom fusion | bytes 4195328 | tf_op jit(solution)/shard_map/jit(_take)/gather | solution.py:70
  129.4 8.3 %fusion.10 = (f32[256]{0:T(256)S(1)}, f32[256]{0:T(256)S(1)}, f32[256,4096]{1,0:T(8,128)}) fusion(bf16[256,4096]{1,0:T(8,128)(2,1)S(1)} %gather_fusion.1, pred[256]{0:T(512)(128)(4,1)S(1)} %get-tuple-element.5, pred[256]{0:T(512)(128)(4,1)S(1)} %iota_compare_fusion.5, f32[4096]{0:T(1024)S(1)} %copy-done.4, bf16[256,1024]{1,0:T(8,128)(2,1)S(1)} %copy-done, ...), kind=kOutput, calls=%fused_computation.25 | convolution fusion | flops 2155871744 | bytes 15223296 | tf_op jit(solution)/shard_map/dot_general | solution.py:79
  137.8 8.6 %fusion.13 = f32[4096,1024]{1,0:T(8,128)} fusion(bf16[256,1024]{1,0:T(8,128)(2,1)S(1)} %copy-done, f32[4096]{0:T(1024)S(1)} %copy-done.4, f32[256]{0:T(256)S(1)} %get-tuple-element.10, bf16[256,4096]{1,0:T(8,128)(2,1)S(1)} %gather_fusion.1, pred[256]{0:T(512)(128)(4,1)S(1)} %get-tuple-element.5, pred[256]{0:T(512)(128)(4,1)S(1)} %iota_compare_fusion.5), kind=kOutput, calls=%fused_computation.31 | convolution fusion | flops 2153775104 | bytes 19416576 | tf_op jit(solution)/shard_map/dot_general | solution.py:85
  146.4 8.3 %scatter_custom_fusion.1 = bf16[384,4096]{1,0:T(8,128)(2,1)} fusion(s32[256]{0:T(256)S(1)} %bitcast.64, bf16[]{:T(256)} %constant.57.clone.1, f32[256,4096]{1,0:T(8,128)} %get-tuple-element.13, f32[256]{0:T(256)S(1)} %get-tuple-element.9, f32[256]{0:T(256)S(1)} %get-tuple-element.10, pred[256]{0:T(512)(128)(4,1)S(1)} %iota_compare_fusion.5, ...), kind=kCustom, calls=%fused_computation.28 | custom fusion | flops 9437184 | bytes 9440258 | tf_op jit(solution)/shard_map/scatter | solution.py:96
  154.7 8.9 %all-to-all-start.2 = ((bf16[16,24,4096]{2,1,0:T(8,128)(2,1)}), bf16[16,24,4096]{2,1,0:T(8,128)(2,1)}, u32[]{:S(2)}, u32[]{:S(2)}) async-start(bf16[16,24,4096]{2,1,0:T(8,128)(2,1)} %bitcast.57), calls=%async_computation.3 | async-start | bytes 6291456 | tf_op jit(solution)/shard_map/all_to_all | solution.py:99
  163.8 108.0 %reduce-scatter.2.cloned.1.call-done = f32[256,1024]{1,0:T(8,128)} async-done(((f32[4096,1024]{1,0:T(8,128)}), f32[256,1024]{1,0:T(8,128)}) %reduce-scatter.2.cloned.1.call-update) | async-done | bytes 1048592 | tf_op jit(solution)/shard_map/reduce_scatter | solution.py:84
  271.8 6.6 %convolution_convert_fusion = bf16[256,1024]{1,0:T(8,128)(2,1)} fusion(bf16[4096,1024]{1,0:T(8,128)(2,1)} %all-gather.2.cloned.1.call-done, f32[4096]{0:T(1024)S(1)} %copy-done.4, f32[256]{0:T(256)S(1)} %get-tuple-element.10, bf16[256,4096]{1,0:T(8,128)(2,1)S(1)} %gather_fusion.1, pred[256]{0:T(512)(128)(4,1)S(1)} %get-tuple-element.5, ...), kind=kOutput, calls=%fused_computation.30 | convolution fusion | flops 2154037248 | bytes 11027968 | tf_op jit(solution)/shard_map/dot_general | solution.py:78
  278.5 2.6 convolution_divide_fusion
  281.0 3.7 fusion.4
  284.7 4.3 fusion
  289.0 149.5 %all-reduce.2.cloned.1.call-done = f32[256,1024]{1,0:T(8,128)} async-done(((f32[256,1024]{1,0:T(8,128)}), f32[256,1024]{1,0:T(8,128)}) %all-reduce.2.cloned.1.call-update) | async-done | bytes 1048592 | tf_op jit(solution)/shard_map/psum | solution.py:92
  438.5 2.3 copy.18
  (30 shorter events, 0.7 us)
Async XLA Ops:
  7.2 122.3 %copy-start = (bf16[256,1024]{1,0:T(8,128)(2,1)S(1)}, bf16[256,1024]{1,0:T(8,128)(2,1)}, u32[]{:S(2)}) copy-start(bf16[256,1024]{1,0:T(8,128)(2,1)} %param.17) | copy-start | bytes 1572868
  7.2 22.1 %copy-start.3 = (f32[4096]{0:T(1024)S(1)}, f32[4096]{0:T(1024)}, u32[]{:S(2)}) copy-start(f32[4096]{0:T(1024)} %param.11) | copy-start | bytes 49156
  7.2 122.2 %all-gather.2.cloned.1.call-start = ((), (), s32[]{:S(2)}) async-start(), calls=%async_computation.4 | async-start | bytes 8912896 | tf_op jit(solution)/shard_map/all_gather | solution.py:44
  13.1 21.1 %all-to-all-start = ((s32[16,1,24]{2,1,0:T(1,128)}), s32[16,1,24]{2,1,0:T(1,128)S(1)}, u32[]{:S(2)}, u32[]{:S(2)}) async-start(s32[16,1,24]{2,1,0:T(1,128)} %all_to_all.12), calls=%async_computation | async-start | bytes 16384 | tf_op jit(solution)/shard_map/all_to_all | solution.py:65
  24.4 4.9 %copy-start.1 = (bf16[512,4096]{1,0:T(8,128)(2,1)S(1)}, bf16[512,4096]{1,0:T(8,128)(2,1)}, u32[]{:S(2)}) copy-start(bf16[512,4096]{1,0:T(8,128)(2,1)} %param.9) | copy-start | bytes 12582916
  43.5 79.7 %all-to-all-start.1 = ((bf16[16,24,4096]{2,1,0:T(8,128)(2,1)}), bf16[16,24,4096]{2,1,0:T(8,128)(2,1)}, u32[]{:S(2)}, u32[]{:S(2)}) async-start(bf16[16,24,4096]{2,1,0:T(8,128)(2,1)} %broadcast_select_fusion), calls=%async_computation.1 | async-start | bytes 6291456 | tf_op jit(solution)/shard_map/all_to_all | solution.py:69
  50.4 221.4 %reduce-scatter.2.cloned.1.call-start = ((), (), s32[]{:S(2)}) async-start(), calls=%async_computation.5 | async-start | bytes 17825792 | tf_op jit(solution)/shard_map/reduce_scatter | solution.py:84
  123.2 6.2 %copy-start.4 = (f32[4096]{0:T(1024)S(1)}, f32[4096]{0:T(1024)}, u32[]{:S(2)}) copy-start(f32[4096]{0:T(1024)} %param.15) | copy-start | bytes 49156
  154.7 123.8 %all-to-all-start.2 = ((bf16[16,24,4096]{2,1,0:T(8,128)(2,1)}), bf16[16,24,4096]{2,1,0:T(8,128)(2,1)}, u32[]{:S(2)}, u32[]{:S(2)}) async-start(bf16[16,24,4096]{2,1,0:T(8,128)(2,1)} %bitcast.57), calls=%async_computation.3 | async-start | bytes 6291456 | tf_op jit(solution)/shard_map/all_to_all | solution.py:99
  163.6 274.8 %all-reduce.2.cloned.1.call-start = ((), (), s32[]{:S(2)}) async-start(), calls=%async_computation.6 | async-start | bytes 2097152 | tf_op jit(solution)/shard_map/psum | solution.py:92
  278.5 6.3 %copy-start.2 = (bf16[512,4096]{1,0:T(8,128)(2,1)S(1)}, bf16[512,4096]{1,0:T(8,128)(2,1)}, u32[]{:S(2)}) copy-start(bf16[512,4096]{1,0:T(8,128)(2,1)} %param.9) | copy-start | bytes 12582916
Sparse Core Ops, SparseCore 0:
  9.9 68.8 all-gather.1
  146.5 125.2 reduce-scatter.1
  274.5 163.9 all-reduce.1
where the time goes:
time: 448 us; the launch traced here: 447 us
  waiting for transfers between devices  333 us (74%)
  other arithmetic  30.8 us (7%)
  starting transfers between devices  27.3 us (6%)
  matrix products  26 us (6%)
  local copies, waits for them, and re-layouts  15.6 us (3%)
  between operations  14.6 us (3%)
    psum x1, waiting for transfers between devices, local(): weight_grad = lax.psum(weight_shard, 'dp')  149 us
    reduce_scatter x1, waiting for transfers between devices, local(): lax.psum_scatter(lax.dot_general(hidden, key_grad, (((0,), (0,)), ((), ()...  108 us
    all_to_all x1, waiting for transfers between devices, local(): lax.all_to_all(outgoing, 'dp', split_axis=0, concat_axis=0, tiled=True)  71.9 us
    all_to_all x1, starting transfers between devices, local(): lax.all_to_all(request, 'dp', split_axis=0, concat_axis=0, tiled=True)  11.2 us
  transfers between devices with their start and end apart: 6, of which 4 were waited for; matrix products, arithmetic and copies ran while one was open for 12% of the time, Pallas kernels for 0%

commit v1 on v0

--- a/solution.py
+++ b/solution.py
@@ -1,9 +1,18 @@
+import functools
 import jax
 import jax.numpy as jnp
 from jax import lax
 from jax.sharding import PartitionSpec as P
 
 EPS = 1e-05
+
+
+def raise_the_terms(x_local, device_axis):
+    n_now = lax.all_gather(x_local, device_axis)
+    return jnp.sum(n_now, 0)
+
+
+frames_view = functools.partial(raise_the_terms, device_axis="dp")
 
 
 def rms_scale(vector, gain_row):
@@ -89,7 +98,7 @@
         scatter_dimension=0,
         tiled=True,
     )
-    weight_grad = lax.psum(weight_shard, "dp")
+    weight_grad = frames_view(weight_shard)
     scattered = (
         jnp.zeros((group_count * capacity, model_width), jnp.bfloat16)
         .at[bucket]

time: 448 us -> 555 us (1.24)
  waiting for transfers between devices: 333 us -> 432 us
  other arithmetic: 30.8 us -> 39.4 us
    all_gather x0 -> x1, waiting for transfers between devices: none -> 159 us  [raise_the_terms(): n_now = lax.all_gather(x_local, device_axis)]
    psum x1 -> x0, waiting for transfers between devices: 149 us -> none  [local(): weight_grad = lax.psum(weight_shard, 'dp')]
    all_to_all x1, waiting for transfers between devices: 0.01 us -> 99.7 us  [local(): lax.all_to_all(scattered, 'dp', split_axis=0, concat_axis=0, tiled=True)]
    reduce_scatter x1, waiting for transfers between devices: 108 us -> 98.1 us  [local(): lax.psum_scatter(lax.dot_general(hidden, key_grad, (((0,), (0,)), ((), ()...]
    reduce_sum x0 -> x1, other arithmetic: none -> 8.76 us  [raise_the_terms(): return jnp.sum(n_now, 0)]
  transfers between devices with their start and end apart: 6 -> 6, of which waited for: 4 -> 5; matrix products, arithmetic and copies ran while one was open for 12% -> 10% of each run, Pallas kernels for 0% -> 0%
where the time goes in v1:
time: 555 us; the launch traced here: 554 us
  waiting for transfers between devices  432 us (78%)
  other arithmetic  39.4 us (7%)
  starting transfers between devices  28.4 us (5%)
  matrix products  26.5 us (5%)
  between operations  14.6 us (3%)
  local copies, waits for them, and re-layouts  13.3 us (2%)
    all_gather x1, waiting for transfers between devices, raise_the_terms(): n_now = lax.all_gather(x_local, device_axis)  159 us
    all_to_all x1, waiting for transfers between devices, local(): lax.all_to_all(scattered, 'dp', split_axis=0, concat_axis=0, tiled=True)  99.7 us
    reduce_scatter x1, waiting for transfers between devices, local(): lax.psum_scatter(lax.dot_general(hidden, key_grad, (((0,), (0,)), ((), ()...  98.1 us
    all_to_all x1, waiting for transfers between devices, local(): lax.all_to_all(outgoing, 'dp', split_axis=0, concat_axis=0, tiled=True)  71.9 us
    all_to_all x1, starting transfers between devices, local(): lax.all_to_all(request, 'dp', split_axis=0, concat_axis=0, tiled=True)  11.2 us
  transfers between devices with their start and end apart: 6, of which 5 were waited for; matrix products, arithmetic and copies ran while one was open for 10% of the time, Pallas kernels for 0%

profile of v1, /device:TPU:2, one launch (start us, length us, event | category | flops | bytes accessed | tf_op | source)
XLA Modules:
  0.0 554.0 jit_solution(1006804259427630792)
XLA Ops:
  7.2 0.7 all-gather.4.cloned.1.call-update
  7.9 0.7 fusion.19
  8.6 0.6 reduce-window.6
  9.4 0.8 fusion.18
  10.2 0.7 and_reduce_fusion
  10.9 1.6 scatter_custom_fusion
  12.4 0.7 all_to_all.12
  13.1 11.2 %all-to-all-start = ((s32[16,1,24]{2,1,0:T(1,128)}), s32[16,1,24]{2,1,0:T(1,128)S(1)}, u32[]{:S(2)}, u32[]{:S(2)}) async-start(s32[16,1,24]{2,1,0:T(1,128)} %all_to_all.12), calls=%async_computation | async-start | bytes 16384 | tf_op jit(solution)/shard_map/all_to_all | solution.py:74
  24.4 0.8 convert_element_type.59
  25.2 1.0 fusion.27
  26.2 3.1 multiply_reduce_fusion.1
  29.3 2.1 multiply_reduce_fusion
  31.5 2.8 all-to-all-done
  34.3 0.5 broadcast.177
  34.8 0.7 reduce.13
  35.6 4.0 gather_fusion
  39.5 4.0 broadcast_select_fusion
  43.5 6.9 %all-to-all-start.1 = ((bf16[16,24,4096]{2,1,0:T(8,128)(2,1)}), bf16[16,24,4096]{2,1,0:T(8,128)(2,1)}, u32[]{:S(2)}, u32[]{:S(2)}) async-start(bf16[16,24,4096]{2,1,0:T(8,128)(2,1)} %broadcast_select_fusion), calls=%async_computation.1 | async-start | bytes 6291456 | tf_op jit(solution)/shard_map/all_to_all | solution.py:78
  51.3 71.9 %all-to-all-done.1 = bf16[16,24,4096]{2,1,0:T(8,128)(2,1)} async-done(((bf16[16,24,4096]{2,1,0:T(8,128)(2,1)}), bf16[16,24,4096]{2,1,0:T(8,128)(2,1)}, u32[]{:S(2)}, u32[]{:S(2)}) %all-to-all-start.1) | async-done | bytes 3145760 | tf_op jit(solution)/shard_map/all_to_all | solution.py:78
  123.2 6.2 %gather_fusion.1 = bf16[256,4096]{1,0:T(8,128)(2,1)S(1)} fusion(bf16[384,4096]{1,0:T(8,128)(2,1)} %bitcast.10, s32[1024]{0:T(1024)S(1)} %pad_clamp_fusion), kind=kCustom, calls=%fused_computation.1 | custom fusion | bytes 4195328 | tf_op jit(solution)/shard_map/jit(_take)/gather | solution.py:79
  129.4 8.3 %fusion.10 = (f32[256]{0:T(256)S(1)}, f32[256]{0:T(256)S(1)}, f32[256,4096]{1,0:T(8,128)}) fusion(bf16[256,4096]{1,0:T(8,128)(2,1)S(1)} %gather_fusion.1, pred[256]{0:T(512)(128)(4,1)S(1)} %get-tuple-element.5, pred[256]{0:T(512)(128)(4,1)S(1)} %iota_compare_fusion.5, f32[4096]{0:T(1024)S(1)} %copy-done.5, bf16[256,1024]{1,0:T(8,128)(2,1)S(1)} %copy-done, ...), kind=kOutput, calls=%fused_computation.25 | convolution fusion | flops 2155871744 | bytes 15223296 | tf_op jit(solution)/shard_map/dot_general | solution.py:88
  137.8 8.6 %fusion.13 = f32[4096,1024]{1,0:T(8,128)} fusion(bf16[256,1024]{1,0:T(8,128)(2,1)S(1)} %copy-done, f32[4096]{0:T(1024)S(1)} %copy-done.5, f32[256]{0:T(256)S(1)} %get-tuple-element.10, bf16[256,4096]{1,0:T(8,128)(2,1)S(1)} %gather_fusion.1, pred[256]{0:T(512)(128)(4,1)S(1)} %get-tuple-element.5, pred[256]{0:T(512)(128)(4,1)S(1)} %iota_compare_fusion.5), kind=kOutput, calls=%fused_computation.31 | convolution fusion | flops 2153775104 | bytes 19416576 | tf_op jit(solution)/shard_map/dot_general | solution.py:94
  146.6 98.1 %reduce-scatter.2.cloned.1.call-done = f32[256,1024]{1,0:T(8,128)} async-done(((f32[4096,1024]{1,0:T(8,128)}), f32[256,1024]{1,0:T(8,128)}) %reduce-scatter.2.cloned.1.call-update) | async-done | bytes 1048592 | tf_op jit(solution)/shard_map/reduce_scatter | solution.py:93
  244.8 8.1 %scatter_custom_fusion.1 = bf16[384,4096]{1,0:T(8,128)(2,1)} fusion(s32[256]{0:T(256)S(1)} %bitcast.66, bf16[]{:T(256)} %constant.57.clone.1, f32[256,4096]{1,0:T(8,128)} %get-tuple-element.13, f32[256]{0:T(256)S(1)} %get-tuple-element.9, f32[256]{0:T(256)S(1)} %get-tuple-element.10, pred[256]{0:T(512)(128)(4,1)S(1)} %iota_compare_fusion.5, ...), kind=kCustom, calls=%fused_computation.28 | custom fusion | flops 9437184 | bytes 9440258 | tf_op jit(solution)/shard_map/scatter | solution.py:105
  252.9 9.8 %all-to-all-start.2 = ((bf16[16,24,4096]{2,1,0:T(8,128)(2,1)}), bf16[16,24,4096]{2,1,0:T(8,128)(2,1)}, u32[]{:S(2)}, u32[]{:S(2)}) async-start(bf16[16,24,4096]{2,1,0:T(8,128)(2,1)} %bitcast.59), calls=%async_computation.3 | async-start | bytes 6291456 | tf_op jit(solution)/shard_map/all_to_all | solution.py:108
  262.8 7.0 %convolution_convert_fusion = bf16[256,1024]{1,0:T(8,128)(2,1)} fusion(bf16[4096,1024]{1,0:T(8,128)(2,1)} %all-gather.4.cloned.1.call-done, f32[4096]{0:T(1024)S(1)} %copy-done.5, f32[256]{0:T(256)S(1)} %get-tuple-element.10, bf16[256,4096]{1,0:T(8,128)(2,1)S(1)} %gather_fusion.1, pred[256]{0:T(512)(128)(4,1)S(1)} %get-tuple-element.5, ...), kind=kOutput, calls=%fused_computation.30 | convolution fusion | flops 2154037248 | bytes 11027968 | tf_op jit(solution)/shard_map/dot_general | solution.py:87
  269.8 99.7 %all-to-all-done.2 = bf16[16,24,4096]{2,1,0:T(8,128)(2,1)} async-done(((bf16[16,24,4096]{2,1,0:T(8,128)(2,1)}), bf16[16,24,4096]{2,1,0:T(8,128)(2,1)}, u32[]{:S(2)}, u32[]{:S(2)}) %all-to-all-start.2) | async-done | bytes 3145760 | tf_op jit(solution)/shard_map/all_to_all | solution.py:108
  369.6 2.6 convolution_divide_fusion
  372.1 3.7 fusion.4
  375.8 4.3 fusion
  380.1 158.5 %all-gather.6.cloned.1.call-done = f32[4096,1024]{1,0:T(8,128)} async-done(((f32[256,1024]{1,0:T(8,128)}), f32[4096,1024]{1,0:T(8,128)}) %all-gather.6.cloned.1.call-update) | async-done | bytes 16777232 | tf_op jit(solution)/shard_map/all_gather | solution.py:11
  538.7 8.8 %reduce_sum.78 = f32[256,1024]{1,0:T(8,128)} reduce(f32[16,256,1024]{2,1,0:T(8,128)} %bitcast.57, f32[]{:T(128)} %constant.32.clone.1), dimensions={0}, to_apply=%region_8.9 | reduce | flops 3932160 | bytes 17825796 | tf_op jit(solution)/shard_map/reduce_sum | solution.py:12
  (32 shorter events, 1.2 us)
Async XLA Ops:
  7.2 122.3 %copy-start = (bf16[256,1024]{1,0:T(8,128)(2,1)S(1)}, bf16[256,1024]{1,0:T(8,128)(2,1)}, u32[]{:S(2)}) copy-start(bf16[256,1024]{1,0:T(8,128)(2,1)} %param.17) | copy-start | bytes 1572868
  7.2 22.1 %copy-start.4 = (f32[4096]{0:T(1024)S(1)}, f32[4096]{0:T(1024)}, u32[]{:S(2)}) copy-start(f32[4096]{0:T(1024)} %param.11) | copy-start | bytes 49156
  7.2 122.2 %all-gather.4.cloned.1.call-start = ((), (), s32[]{:S(2)}) async-start(), calls=%async_computation.4 | async-start | bytes 8912896 | tf_op jit(solution)/shard_map/all_gather | solution.py:53
  13.1 21.1 %all-to-all-start = ((s32[16,1,24]{2,1,0:T(1,128)}), s32[16,1,24]{2,1,0:T(1,128)S(1)}, u32[]{:S(2)}, u32[]{:S(2)}) async-start(s32[16,1,24]{2,1,0:T(1,128)} %all_to_all.12), calls=%async_computation | async-start | bytes 16384 | tf_op jit(solution)/shard_map/all_to_all | solution.py:74
  24.4 4.9 copy-start.2
  43.5 79.7 %all-to-all-start.1 = ((bf16[16,24,4096]{2,1,0:T(8,128)(2,1)}), bf16[16,24,4096]{2,1,0:T(8,128)(2,1)}, u32[]{:S(2)}, u32[]{:S(2)}) async-start(bf16[16,24,4096]{2,1,0:T(8,128)(2,1)} %broadcast_select_fusion), calls=%async_computation.1 | async-start | bytes 6291456 | tf_op jit(solution)/shard_map/all_to_all | solution.py:78
  50.4 194.4 %reduce-scatter.2.cloned.1.call-start = ((), (), s32[]{:S(2)}) async-start(), calls=%async_computation.5 | async-start | bytes 17825792 | tf_op jit(solution)/shard_map/reduce_scatter | solution.py:93
  123.2 6.2 %copy-start.5 = (f32[4096]{0:T(1024)S(1)}, f32[4096]{0:T(1024)}, u32[]{:S(2)}) copy-start(f32[4096]{0:T(1024)} %param.15) | copy-start | bytes 49156
  146.4 392.3 %all-gather.6.cloned.1.call-start = ((), (), s32[]{:S(2)}) async-start(), calls=%async_computation.6 | async-start | bytes 17825792 | tf_op jit(solution)/shard_map/all_gather | solution.py:11
  252.9 116.7 %all-to-all-start.2 = ((bf16[16,24,4096]{2,1,0:T(8,128)(2,1)}), bf16[16,24,4096]{2,1,0:T(8,128)(2,1)}, u32[]{:S(2)}, u32[]{:S(2)}) async-start(bf16[16,24,4096]{2,1,0:T(8,128)(2,1)} %bitcast.59), calls=%async_computation.3 | async-start | bytes 6291456 | tf_op jit(solution)/shard_map/all_to_all | solution.py:108
  369.6 6.3 %copy-start.3 = (bf16[512,4096]{1,0:T(8,128)(2,1)S(1)}, bf16[512,4096]{1,0:T(8,128)(2,1)}, u32[]{:S(2)}) copy-start(bf16[512,4096]{1,0:T(8,128)(2,1)} %param.9) | copy-start | bytes 12582916
  538.7 8.8 %copy-start.1 = (bf16[256,1024]{1,0:T(8,128)(2,1)S(1)}, bf16[256,1024]{1,0:T(8,128)(2,1)}, u32[]{:S(2)}) copy-start(bf16[256,1024]{1,0:T(8,128)(2,1)} %param.17) | copy-start | bytes 1572868
Sparse Core Ops, SparseCore 0:
  9.8 68.8 all-gather.3
  146.5 98.2 reduce-scatter.1
  247.3 291.2 all-gather.5
